TPU v7x, 512 devices: a whole 4x4x16 slice. The times are simulated.
512 devices in a mesh: row: 16 (over z), col: 32 (over x, y, core).
Axes of the slice: x: 4, y: 4, z: 16, core: 2. Of those that a mesh axis runs over, the one named last changes fastest.
Arguments:
- panel: float32 [4, 1536, 1, 32, 1536], P(None, 'row', None, 'col'), may hold values from -1 to 1, as said below
- inverse_blocks: float32 [4, 1536, 1536], P(None, 'row'), may hold values from -1 to 2, as said below
- right_side: float32 [48, 1, 32, 1536], P(None, None, 'col'), may hold values from -6 to 6
Outputs:
- solved: float32 [48, 4, 1536], P(None, None, 'row')
- updated: float32 [48, 1, 32, 1536], P(None, None, 'col', 'row')
Inputs may be any that keep to these rules, and one draw needn't show every extreme that they name: panel is zero where the row index is below the column index as defined in its meaning (the factor is lower triangular). `inverse_blocks`: each inverse block is lower triangular with a positive diagonal.
All inputs are finite; a program needn't handle non-finite values.
Results may differ from a plain program's by a relative error of at most 0.0001.
Values sent between devices are 32-bit elements; how exact they have to be, the bound alone decides.
A program may use at most 64 MiB of HBM per device.

v0:
```python
import jax
import jax.numpy as jnp
from jax import lax
from jax.sharding import PartitionSpec as P


def broadcast(value, axis, source):
    kept = jnp.where(lax.axis_index(axis) == source, value, 0).astype(value.dtype)
    return lax.psum(kept, axis)


def body(panel, inverse_blocks, right_side):
    steps = panel.shape[0]
    row_index = lax.axis_index("row")
    heads = right_side[:, 0, 0, :]
    count_rhs = right_side.shape[0]
    count_rowblk = right_side.shape[1]
    block_len = right_side.shape[3]
    accum = jnp.zeros((count_rhs, count_rowblk, block_len), jnp.float32)
    solved_list = []
    for step in range(steps):
        partial_value = accum[:, 0, :]
        residue = heads - lax.psum(partial_value, "row")
        own_piece = jnp.dot(
            residue,
            inverse_blocks[step].T,
            precision=lax.Precision.HIGHEST,
            preferred_element_type=jnp.float32,
        )
        piece = broadcast(own_piece, "col", step)
        solved_list.append(piece)
        columns = panel[step, :, :, 0, :]
        accum = accum + jnp.einsum("rc,cji->rji", piece, columns, precision=lax.Precision.HIGHEST)
    totals = lax.psum_scatter(accum, "row", scatter_dimension=2, tiled=True)
    slice_len = totals.shape[2]
    mine = lax.dynamic_slice_in_dim(right_side, row_index * slice_len, slice_len, 3)[:, :, 0, :]
    updated = (mine - totals)[:, :, None, :]
    solved = jnp.stack(solved_list, axis=1)
    return (solved, updated)


def solution(mesh):
    placed = (P(None, "row", None, "col", None), P(None, "row", None), P(None, None, "col", None))
    return jax.shard_map(
        body,
        mesh=mesh,
        in_specs=placed,
        out_specs=(P(None, None, "row"), P(None, None, "col", "row")),
        check_vma=False,
    )
```

profile of v0, /device:TPU:6, one launch (start us, length us, event | category | flops | bytes accessed | tf_op | source)
XLA Modules:
  0.0 984.7 jit_solution(11733862175984797096)
XLA Ops:
  7.2 1.9 convolution_select_fusion.3
  9.1 110.5 %psum.52 = f32[48,96]{1,0:T(8,128)S(1)} all-reduce(f32[48,96]{1,0:T(8,128)S(1)} %convolution_select_fusion.3), channel_id=1, replica_groups=mesh['row'=16,'col'=32] {'col'}, use_global_device_ids=true, to_apply=%region_0.0 | all-reduce | flops 4608 | bytes 36864 | tf_op jit(solution)/shard_map/psum | solution.py:9
  119.6 2.9 fusion.23
  122.5 1.1 fusion.7
  123.7 0.0 all-reduce.6.cloned.1.call-start
  123.8 153.2 %all-reduce.4.cloned.1.call-done = f32[48,1536]{1,0:T(8,128)} async-done(((f32[48,1536]{1,0:T(8,128)}), f32[48,1536]{1,0:T(8,128)}) %all-reduce.4.cloned.1.call-update) | async-done | bytes 294928 | tf_op jit(solution)/shard_map/psum | solution.py:23
  277.0 1.9 convolution_select_fusion.2
  278.9 105.2 %psum.54 = f32[48,96]{1,0:T(8,128)S(1)} all-reduce(f32[48,96]{1,0:T(8,128)S(1)} %convolution_select_fusion.2), channel_id=1, replica_groups=mesh['row'=16,'col'=32] {'col'}, use_global_device_ids=true, to_apply=%region_2.3 | all-reduce | flops 4608 | bytes 36864 | tf_op jit(solution)/shard_map/psum | solution.py:9
  384.1 2.1 convolution_add_fusion.2
  386.2 0.0 all-reduce.8.cloned.1.call-start
  386.3 145.7 %all-reduce.6.cloned.1.call-done = f32[48,1536]{1,0:T(8,128)} async-done(((f32[48,1536]{1,0:T(8,128)}), f32[48,1536]{1,0:T(8,128)}) %all-reduce.6.cloned.1.call-update) | async-done | bytes 294928 | tf_op jit(solution)/shard_map/psum | solution.py:23
  531.9 1.9 convolution_select_fusion.1
  533.8 105.2 %psum.56 = f32[48,96]{1,0:T(8,128)S(1)} all-reduce(f32[48,96]{1,0:T(8,128)S(1)} %convolution_select_fusion.1), channel_id=1, replica_groups=mesh['row'=16,'col'=32] {'col'}, use_global_device_ids=true, to_apply=%region_4.5 | all-reduce | flops 4608 | bytes 36864 | tf_op jit(solution)/shard_map/psum | solution.py:9
  639.0 2.1 convolution_add_fusion.1
  641.2 145.8 %all-reduce.8.cloned.1.call-done = f32[48,1536]{1,0:T(8,128)} async-done(((f32[48,1536]{1,0:T(8,128)}), f32[48,1536]{1,0:T(8,128)}) %all-reduce.8.cloned.1.call-update) | async-done | bytes 294928 | tf_op jit(solution)/shard_map/psum | solution.py:23
  787.0 1.9 convolution_select_fusion
  788.9 105.2 %psum.58 = f32[48,96]{1,0:T(8,128)S(1)} all-reduce(f32[48,96]{1,0:T(8,128)S(1)} %convolution_select_fusion), channel_id=1, replica_groups=mesh['row'=16,'col'=32] {'col'}, use_global_device_ids=true, to_apply=%region_6.7 | all-reduce | flops 4608 | bytes 36864 | tf_op jit(solution)/shard_map/psum | solution.py:9
  894.0 1.4 fusion
  895.4 1.7 copy.9
  897.2 0.1 constant_dynamic-slice_fusion
  897.3 0.7 copy.7
  898.0 78.7 %reduce-scatter.4.cloned.1.call-done = f32[96,48]{1,0:T(8,128)} async-done(((f32[1536,48]{1,0:T(8,128)}), f32[96,48]{1,0:T(8,128)}) %reduce-scatter.4.cloned.1.call-update) | async-done | bytes 18448
  976.7 0.9 copy.10
  977.6 0.6 sub.16
  (9 shorter events, 0.2 us)
Async XLA Ops:
  7.2 269.8 %all-reduce.4.cloned.1.call-start = ((), (), s32[]{:S(2)}) async-start(), calls=%async_computation.1 | async-start | bytes 589824 | tf_op jit(solution)/shard_map/psum | solution.py:23
  119.6 157.4 %copy-start = (f32[48,1,1,1536]{3,2,1,0:T(1,128)S(1)}, f32[48,1,1,1536]{3,2,1,0:T(1,128)}, u32[]{:S(2)}) copy-start(f32[48,1,1,1536]{3,2,1,0:T(1,128)} %param.5) | copy-start | bytes 884740
  123.7 408.2 %all-reduce.6.cloned.1.call-start = ((), (), s32[]{:S(2)}) async-start(), calls=%async_computation.2 | async-start | bytes 589824 | tf_op jit(solution)/shard_map/psum | solution.py:23
  386.2 400.8 %all-reduce.8.cloned.1.call-start = ((), (), s32[]{:S(2)}) async-start(), calls=%async_computation.3 | async-start | bytes 589824 | tf_op jit(solution)/shard_map/psum | solution.py:23
  641.1 335.6 %reduce-scatter.4.cloned.1.call-start = ((), (), s32[]{:S(2)}) async-start(), calls=%async_computation.4 | async-start | bytes 835584
Sparse Core Ops, SparseCore 0:
  123.8 153.1 all-reduce.3
  386.3 145.5 all-reduce.5
  641.3 145.6 all-reduce.7
  897.3 79.3 reduce-scatter.3
where the time goes:
time: 985 us
  waiting for transfers between devices  524 us (53%)
  blocking collectives  426 us (43%)
  matrix products  14.3 us (1%)
  between operations  13.9 us (1%)
    psum x3, waiting for transfers between devices, body(): residue = heads - lax.psum(partial_value, 'row')  445 us
    psum x4, blocking collectives, broadcast(): return lax.psum(kept, axis)  426 us
    unnamed x5, waiting for transfers between devices  78.8 us
  transfers between devices with their start and end apart: 4, of which 4 were waited for; matrix products, arithmetic and copies ran while one was open for 0% of the time, Pallas kernels for 0%

commit v1 on v0

v1 whole, which is shorter than its diff:
```python
import jax
import jax.numpy as jnp
from jax import lax
from jax.experimental import pallas as pl
from jax.experimental.pallas import tpu as pltpu
from jax.sharding import PartitionSpec as P

MESH = pl.DeviceIdType.MESH
F32 = jnp.float32
HI = lax.Precision.HIGHEST
ROWS, COLS = 16, 32
STEPS, RHS, BLK, SLC = 4, 48, 1536, 96
TILES = BLK // 128
CHAIN = (4, 6, 8, 10, 24, 26)
PART = RHS // len(CHAIN)
CUT = BLK // 4


def dot(left, right):
    return lax.dot_general(left, right, (((1,), (0,)), ((), ())), precision=HI, preferred_element_type=F32)


def dot_t(left, right):
    return lax.dot_general(left, right, (((1,), (1,)), ((), ())), precision=HI, preferred_element_type=F32)


def kernel(
    panel_ref,
    inverse_ref,
    right_ref,
    solved_ref,
    updated_ref,
    flat,
    cut,
    rep_flat,
    inv,
    right_flat,
    right,
    pieces,
    base,
    base_in,
    rs_out,
    rs_in,
    residue,
    mine,
    acc,
    packed,
    fin_in,
    load_sem,
    rep_send,
    rep_recv,
    piece_send,
    piece_recv,
    base_send,
    base_recv,
    rs_send,
    rs_recv,
    ag_send,
    ag_recv,
    fin_send,
    fin_recv,
):
    p = lax.axis_index("row")
    q = lax.axis_index("col")
    is_chain = q == CHAIN[0]
    g = jnp.int32(0)
    for n, c in enumerate(CHAIN):
        is_chain = is_chain | (q == c)
        g = g + jnp.where(q == c, n, 0)

    def wait(ref, sem):
        pltpu.make_async_copy(ref, ref, sem).wait()

    def push(src, dst, send, recv, where):
        pltpu.make_async_remote_copy(
            src_ref=src, dst_ref=dst, send_sem=send, recv_sem=recv, device_id=where, device_id_type=MESH
        ).start()

    load_right = pltpu.make_async_copy(right_ref, right_flat, load_sem.at[0])
    load_panel = pltpu.make_async_copy(panel_ref, flat, load_sem.at[1])
    load_inv = pltpu.make_async_copy(inverse_ref, inv, load_sem.at[2])
    load_right.start()
    load_inv.start()
    load_panel.start()

    barrier = pltpu.get_barrier_semaphore()

    def hello_plane(i, _):
        pl.semaphore_signal(barrier, inc=1, device_id=(p, lax.rem(q + i, COLS)), device_id_type=MESH)
        return 0

    def hello_ring(i, _):
        pl.semaphore_signal(barrier, inc=1, device_id=(lax.rem(p + i, ROWS), q), device_id_type=MESH)
        return 0

    lax.fori_loop(1, ROWS, hello_ring, 0)
    lax.fori_loop(1, COLS, hello_plane, 0)

    load_right.wait()
    for j in range(TILES):
        right[:, 128 * j : 128 * (j + 1)] = right_flat[pl.ds(j, RHS, stride=TILES), :]
    load_inv.wait()

    @pl.when(q == 0)
    def _():
        first = dot_t(right[...], inv[0])
        pieces[0, :, 0:SLC] = first

    pl.semaphore_wait(barrier, ROWS - 1 + COLS - 1)
    load_panel.wait()

    def spread_first(i, _):
        push(pieces.at[0], pieces.at[0], piece_send.at[0], piece_recv.at[0], (p, lax.rem(q + i, COLS)))
        return 0

    @pl.when(q == 0)
    def _():
        lax.fori_loop(1, COLS, spread_first, 0)

    for k in (2, 3):

        @pl.when(q == k)
        def _():
            for n, c in enumerate(CHAIN):
                push(
                    flat.at[pl.ds((k - 1) * SLC * TILES, SLC * TILES)],
                    rep_flat.at[k - 2],
                    rep_send.at[n],
                    rep_recv.at[k - 2],
                    (p, c),
                )

    def panel_block(k):
        return [flat[pl.ds(k * SLC * TILES + j, SLC, stride=TILES), :] for j in range(TILES)]

    def send_base(k):
        for n, c in enumerate(CHAIN):
            push(
                base.at[pl.ds(PART * n, PART)],
                base_in.at[k - 1],
                base_send.at[0],
                base_recv.at[k - 1],
                (p, c),
            )

    own = jnp.where(p == 0, 1.0, 0.0).astype(F32)

    @pl.when(q == 1)
    def _():
        wait(pieces.at[0], piece_recv.at[0])
        for j, block in enumerate(panel_block(0)):
            at = slice(128 * j, 128 * (j + 1))
            base[:, at] = own * right[:, at] - dot(pieces[0, :, 0:SLC], block)
        send_base(1)

    lane = lax.broadcasted_iota(jnp.int32, (SLC, 128), 1)

    def cut_block(k, _):
        for n in range(ROWS):
            tile, shift = (SLC * n) // 128, (SLC * n) % 128
            block = flat[pl.ds(k * SLC * TILES + tile, SLC, stride=TILES), :]
            if shift:
                block = pltpu.roll(block, 128 - shift, 1)
                if shift > 128 - SLC:
                    after = flat[pl.ds(k * SLC * TILES + tile + 1, SLC, stride=TILES), :]
                    block = jnp.where(lane < 128 - shift, block, pltpu.roll(after, 128 - shift, 1))
            cut[k, :, 128 * n : 128 * (n + 1)] = block
        return 0

    lax.fori_loop(0, STEPS, cut_block, 0)

    def add_piece(k):
        piece = pieces[k, :, 0:SLC]
        for n in range(0, ROWS, 2):
            term = dot(piece, cut[k, :, 128 * n : 128 * (n + 2)])
            for h in range(2):
                value = term[:, 128 * h : 128 * (h + 1)]
                if k == 0:
                    acc[n + h] = value
                else:
                    acc[n + h] += value

    @pl.when(q == 2)
    def _():
        wait(pieces.at[0], piece_recv.at[0])
        for j, block in enumerate(panel_block(0)):
            at = slice(128 * j, 128 * (j + 1))
            base[:, at] = own * right[:, at] - dot(pieces[0, :, 0:SLC], block)
        send_base(2)

    @pl.when(q == 3)
    def _():
        wait(pieces.at[0], piece_recv.at[0])
        wait(pieces.at[1], piece_recv.at[1])
        first, second = panel_block(0), panel_block(1)
        for j in range(TILES):
            at = slice(128 * j, 128 * (j + 1))
            term = dot(pieces[0, :, 0:SLC], first[j]) + dot(pieces[1, :, 0:SLC], second[j])
            base[:, at] = own * right[:, at] - term
        send_base(3)

    def far_first(i):
        return lax.rem(p + 8 + (1 - 2 * lax.rem(i, 2)) * lax.div(i + 1, 2), ROWS)

    @pl.when(is_chain)
    def _():
        rows = pl.ds(pl.multiple_of(PART * g, PART), PART)
        my_cut = pl.ds(pl.multiple_of(CUT * lax.rem(p, 4), 128), CUT)

        def spread(k):
            def send(i, _):
                push(
                    mine.at[k],
                    pieces.at[k, rows],
                    piece_send.at[k],
                    piece_recv.at[k],
                    (p, lax.rem(q + i, COLS)),
                )
                return 0

            lax.fori_loop(1, COLS, send, 0)

        for k in range(1, STEPS):
            wait(base_in.at[k - 1], base_recv.at[k - 1])
            if k == 1:
                rs_out[0] = base_in[0]
            else:
                wait(rep_flat.at[k - 2], rep_recv.at[k - 2])
                for j in range(TILES):
                    at = slice(128 * j, 128 * (j + 1))
                    block = rep_flat[k - 2, pl.ds(j, SLC, stride=TILES), :]
                    rs_out[k - 1, :, at] = base_in[k - 1, :, at] - dot(mine[k - 1, :, 0:SLC], block)

            def scatter(i, _):
                to = far_first(i)
                part = pl.ds(pl.multiple_of(CUT * lax.rem(to, 4), 128), CUT)
                slot = lax.rem(p - to + ROWS, ROWS) - 1
                push(
                    rs_out.at[k - 1, :, part],
                    rs_in.at[k - 1, slot],
                    rs_send.at[k - 1],
                    rs_recv.at[k - 1],
                    (to, q),
                )
                return 0

            lax.fori_loop(0, ROWS - 1, scatter, 0)
            if k == 1:
                wait(pieces.at[0], piece_recv.at[0])
            else:
                spread(k - 1)
                wait(pieces.at[k - 1, pl.ds(0, RHS - PART)], piece_recv.at[k - 1])
                pieces[k - 1, rows, :] = mine[k - 1]
            add_piece(k - 1)

            wait(rs_in.at[k - 1], rs_recv.at[k - 1])
            total = rs_out[k - 1, :, my_cut]
            for n in range(ROWS - 1):
                total = total + rs_in[k - 1, n]
            residue[k - 1, :, my_cut] = total
            for d in (2, -1, 1):
                push(
                    residue.at[k - 1, :, my_cut],
                    residue.at[k - 1, :, my_cut],
                    ag_send.at[k - 1],
                    ag_recv.at[k - 1],
                    (lax.rem(p - d + ROWS, ROWS), q),
                )
            wait(residue.at[k - 1, :, pl.ds(0, 3 * CUT)], ag_recv.at[k - 1])
            mine[k, :, 0:SLC] = dot_t(residue[k - 1], inv[k])
            mine[k, :, SLC:] = jnp.zeros((PART, 128 - SLC), F32)

        spread(STEPS - 1)
        last = STEPS - 1
        wait(pieces.at[last, pl.ds(0, RHS - PART)], piece_recv.at[last])
        pieces[last, rows, :] = mine[last]

    @pl.when(jnp.logical_not(is_chain))
    def _():
        @pl.when(q > 3)
        def _():
            wait(pieces.at[0], piece_recv.at[0])

        add_piece(0)

        @pl.when(q != 3)
        def _():
            wait(pieces.at[1], piece_recv.at[1])

        add_piece(1)
        wait(pieces.at[2], piece_recv.at[2])
        add_piece(2)
        wait(pieces.at[3], piece_recv.at[3])

    add_piece(STEPS - 1)

    wide = lax.broadcasted_iota(jnp.int32, (8, 128), 1)
    for n in range(ROWS):
        rest = acc[n, RHS - 8 : RHS, :]
        for a in range(3):
            beside = pltpu.roll(rest, SLC - 32 * a, 1)
            packed[n, 8 * a : 8 * (a + 1), :] = jnp.where(wide < SLC, acc[n, 8 * a : 8 * (a + 1), :], beside)
        packed[n, 24 : RHS - 8, :] = acc[n, 24 : RHS - 8, :]

    def finish(i, _):
        to = far_first(i)
        slot = lax.rem(p - to + ROWS, ROWS) - 1
        push(
            packed.at[to],
            fin_in.at[slot],
            fin_send,
            fin_recv,
            (to, q),
        )
        return 0

    lax.fori_loop(0, ROWS - 1, finish, 0)
    for k in range(STEPS):
        solved_ref[:, k, :] = pieces[k, :, 0:SLC]

    tile = lax.div(3 * p, 4)
    shift = 32 * lax.rem(3 * p, 4)
    here = right[:, pl.ds(pl.multiple_of(128 * tile, 128), 128)]
    after = right[:, pl.ds(pl.multiple_of(128 * jnp.minimum(tile + 1, TILES - 1), 128), 128)]
    turn = lax.rem(128 - shift, 128)
    lanes = lax.broadcasted_iota(jnp.int32, (RHS, 128), 1)
    total = jnp.where(lanes < 128 - shift, pltpu.roll(here, turn, 1), pltpu.roll(after, turn, 1))
    term = packed[p]
    wait(fin_in, fin_recv)
    for n in range(ROWS - 1):
        term = term + fin_in[n]
    updated_ref[0 : RHS - 8, :] = (total[0 : RHS - 8, :] - term)[:, 0:SLC]
    last = jnp.where(wide < 32, pltpu.roll(term[0:8, :], 32, 1), pltpu.roll(term[8:16, :], 64, 1))
    last = jnp.where(wide < 64, last, pltpu.roll(term[16:24, :], SLC, 1))
    updated_ref[RHS - 8 : RHS, :] = (total[RHS - 8 : RHS, :] - last)[:, 0:SLC]

    wait(fin_in, fin_send)

    @pl.when(q == 0)
    def _():
        wait(flat.at[pl.ds(0, (COLS - 1) * RHS)], piece_send.at[0])

    @pl.when((q == 2) | (q == 3))
    def _():
        for n in range(len(CHAIN)):
            wait(rep_flat.at[0], rep_send.at[n])

    @pl.when((q >= 1) & (q <= 3))
    def _():
        wait(base, base_send.at[0])

    @pl.when(is_chain)
    def _():
        for k in range(1, STEPS):
            wait(rs_in.at[k - 1], rs_send.at[k - 1])
            wait(residue.at[k - 1, :, pl.ds(0, 3 * CUT)], ag_send.at[k - 1])
            wait(flat.at[pl.ds(0, (COLS - 1) * PART)], piece_send.at[k])


def body(panel, inverse_blocks, right_side):
    hbm = pl.BlockSpec(memory_space=pl.ANY)
    vmem = pl.BlockSpec(memory_space=pltpu.VMEM)
    dma = pltpu.SemaphoreType.DMA
    solved, updated = pl.pallas_call(
        kernel,
        out_shape=(
            jax.ShapeDtypeStruct((RHS, STEPS, SLC), F32),
            jax.ShapeDtypeStruct((RHS, SLC), F32),
        ),
        in_specs=[hbm, hbm, hbm],
        out_specs=(vmem, vmem),
        scratch_shapes=[
            pltpu.VMEM((STEPS * SLC * TILES, 128), F32),
            pltpu.VMEM((STEPS, SLC, ROWS * 128), F32),
            pltpu.VMEM((2, SLC * TILES, 128), F32),
            pltpu.VMEM((STEPS, SLC, BLK), F32),
            pltpu.VMEM((RHS * TILES, 128), F32),
            pltpu.VMEM((RHS, BLK), F32),
            pltpu.VMEM((STEPS, RHS, 128), F32),
            pltpu.VMEM((RHS, BLK), F32),
            pltpu.VMEM((3, PART, BLK), F32),
            pltpu.VMEM((3, PART, BLK), F32),
            pltpu.VMEM((3, ROWS - 1, PART, CUT), F32),
            pltpu.VMEM((3, PART, BLK), F32),
            pltpu.VMEM((STEPS, PART, 128), F32),
            pltpu.VMEM((ROWS, RHS, 128), F32),
            pltpu.VMEM((ROWS, RHS - 8, 128), F32),
            pltpu.VMEM((ROWS - 1, RHS - 8, 128), F32),
            dma((3,)),
            dma((len(CHAIN),)),
            dma((2,)),
            dma((STEPS,)),
            dma((STEPS,)),
            dma((1,)),
            dma((3,)),
            dma((3,)),
            dma((3,)),
            dma((3,)),
            dma((3,)),
            dma,
            dma,
        ],
        compiler_params=pltpu.CompilerParams(
            collective_id=0, has_side_effects=True
        ),
        name="solve",
    )(
        panel.reshape(STEPS * SLC * TILES, 128),
        inverse_blocks,
        right_side.reshape(RHS * TILES, 128),
    )
    return solved, updated.reshape(RHS, 1, 1, SLC)


def solution(mesh):
    placed = (P(None, "row", None, "col", None), P(None, "row", None), P(None, None, "col", None))
    return jax.shard_map(
        body,
        mesh=mesh,
        in_specs=placed,
        out_specs=(P(None, None, "row"), P(None, None, "col", "row")),
        check_vma=False,
    )
```

time: 985 us -> 97.7 us (0.10)
  waiting for transfers between devices: 524 us -> 0 us
  blocking collectives: 426 us -> 0 us
  Pallas kernels: 0 us -> 93.4 us
  matrix products: 14.3 us -> 0 us
  between operations: 13.9 us -> 0.64 us
    psum x3 -> x0, waiting for transfers between devices: 445 us -> none  [body(): residue = heads - lax.psum(partial_value, 'row')]
    psum x4 -> x0, blocking collectives: 426 us -> none  [broadcast(): return lax.psum(kept, axis)]
    pallas_call x0 -> x1, Pallas kernels: none -> 93.4 us  [body(): pl.pallas_call(kernel, out_shape=(jax.ShapeDtypeStruct((RHS, STEPS, SLC),...]
    unnamed x5 -> x0, waiting for transfers between devices: 78.8 us -> none
    dot_general x8 -> x0, matrix products: 14.3 us -> none  [the longest x4 7.55 us: body(): jnp.dot(residue, inverse_blocks[step].T, precision=lax.Precision.HIGHEST,...]
  transfers between devices with their start and end apart: 4 -> 0, of which waited for: 4 -> 0; matrix products, arithmetic and copies ran while one was open for 0% -> 0% of each run, Pallas kernels for 0% -> 0%
where the time goes in v1:
time: 97.7 us; the launch traced here: 96.9 us
  Pallas kernels  93.4 us (96%)
  local copies, waits for them, and re-layouts  2.89 us (3%)
    pallas_call x1, Pallas kernels, body(): pl.pallas_call(kernel, out_shape=(jax.ShapeDtypeStruct((RHS, STEPS, SLC),...  93.4 us
    unnamed x2, local copies, waits for them, and re-layouts  2.89 us

profile of v1, /device:TPU:6, one launch (start us, length us, event | category | flops | bytes accessed | tf_op | source)
XLA Modules:
  0.0 96.9 jit_solution(7553527326527950269)
XLA Ops:
  0.6 93.4 %solve.1 = (f32[48,4,96]{2,1,0:T(4,128)}, f32[48,96]{1,0:T(8,128)}) custom-call(f32[4608,128]{1,0:T(8,128)} %bitcast.5, f32[4,96,1536]{2,1,0:T(8,128)} %inverse_ref.1, f32[576,128]{1,0:T(8,128)} %bitcast.6), custom_call_target="tpu_custom_call" | custom-call | tf_op jit(solution)/shard_map/solve/pallas_call | solution.py:364
  94.1 1.5 %copy.8 = f32[48,4,96]{2,1,0:T(4,128)} copy(f32[48,4,96]{2,1,0:T(4,128)} %get-tuple-element.10) | data formatting | bytes 147456
  95.6 1.3 %copy.9 = f32[48,1,1,96]{3,2,1,0:T(1,128)} copy(f32[48,1,1,96]{3,2,1,0:T(1,128)} %bitcast.7) | data formatting | bytes 36864

commit v2 on v1

v2 whole, which is shorter than its diff:
```python
import jax
import jax.numpy as jnp
from jax import lax
from jax.experimental import pallas as pl
from jax.experimental.pallas import tpu as pltpu
from jax.sharding import PartitionSpec as P

MESH = pl.DeviceIdType.MESH
F32 = jnp.float32
BF16 = jnp.bfloat16
ROWS, COLS = 16, 32
STEPS, RHS, BLK, SLC = 4, 48, 1536, 96
TILES = BLK // 128
CHAIN = (4, 6, 8, 10, 24, 26)
PART = RHS // len(CHAIN)
CUT = BLK // 4
ORDER = (2, 4, 6, 8, 14, 12, 10, 1, 3, 5, 7, 15, 13, 11, 9, 0)


def split(value):
    high = value.astype(BF16)
    return high, (value - high.astype(F32)).astype(BF16)


def dot3(left, right, axis):
    rows = left.shape[0]
    high, low = split(left)
    dims = (((1,), (axis,)), ((), ()))
    both = lax.dot_general(jnp.concatenate([high, low], 0), right[0], dims, preferred_element_type=F32)
    rest = lax.dot_general(high, right[1], dims, preferred_element_type=F32)
    return both[:rows] + (both[rows:] + rest)


def kernel(
    panel_ref,
    inverse_ref,
    right_ref,
    solved_ref,
    updated_ref,
    flat,
    cut_high,
    cut_low,
    rep_flat,
    block_high,
    block_low,
    inv,
    inv_high,
    inv_low,
    right_flat,
    right,
    pieces,
    base,
    base_in,
    rs_out,
    rs_in,
    residue,
    mine,
    acc,
    packed,
    near_in,
    far_in,
    panel_sem,
    inverse_sem,
    right_sem,
    rep_send,
    rep_recv,
    rep_turn,
    first_send,
    piece_send,
    piece_recv,
    base_send,
    base_recv,
    rs_send,
    rs_recv,
    ag_send,
    ag_recv,
    near_send,
    near_recv,
    far_send,
    far_recv,
):
    p = lax.axis_index("row")
    q = lax.axis_index("col")
    is_chain = q == CHAIN[0]
    g = jnp.int32(0)
    for n, c in enumerate(CHAIN):
        is_chain = is_chain | (q == c)
        g = g + jnp.where(q == c, n, 0)

    def wait(ref, sem):
        pltpu.make_async_copy(ref, ref, sem).wait()

    def push(src, dst, send, recv, where):
        pltpu.make_async_remote_copy(
            src_ref=src, dst_ref=dst, send_sem=send, recv_sem=recv, device_id=where, device_id_type=MESH
        ).start()

    def load_inverse(k):
        return pltpu.make_async_copy(inverse_ref.at[k], inv.at[k], inverse_sem.at[k])

    def load_panel(k):
        part = pl.ds(k * SLC * TILES, SLC * TILES)
        return pltpu.make_async_copy(panel_ref.at[part], flat.at[part], panel_sem.at[k])

    load_right = pltpu.make_async_copy(right_ref, right_flat, right_sem)
    load_right.start()

    @pl.when(q == 0)
    def _():
        load_inverse(0).start()

    for k in range(STEPS):
        load_panel(k).start()

    barrier = pltpu.get_barrier_semaphore()

    def hello(row, col):
        pl.semaphore_signal(barrier, inc=1, device_id=(row, col), device_id_type=MESH)

    @pl.when(q == 1)
    def _():
        hello(p, 0)

    @pl.when(is_chain | (q == 3))
    def _():
        hello(p, 1)
        hello(p, 2)

    for c in CHAIN:

        @pl.when(q != c)
        def _():
            hello(p, c)

    @pl.when((q == 2) | (q > 3))
    def _():
        hello(p, 3)

    @pl.when(q > 3)
    def _():
        def ring(i, _):
            hello(lax.rem(p + i, ROWS), q)
            return 0

        lax.fori_loop(1, ROWS, ring, 0)

    @pl.when(is_chain)
    def _():
        for k in range(1, STEPS):
            load_inverse(k).start()

    load_right.wait()
    for j in range(TILES):
        right[:, 128 * j : 128 * (j + 1)] = right_flat[pl.ds(j, RHS, stride=TILES), :]

    def panel_tile(k, j):
        return flat[pl.ds(k * SLC * TILES + j, SLC, stride=TILES), :]

    def split_block(n, tile):
        for j in range(TILES):
            at = slice(128 * j, 128 * (j + 1))
            block_high[n, :, at], block_low[n, :, at] = split(tile(j))

    own = jnp.where(p == 0, 1.0, 0.0).astype(F32)

    def send_base(k):
        for n, c in enumerate(CHAIN):
            push(
                base.at[pl.ds(PART * n, PART)],
                base_in.at[k - 1],
                base_send,
                base_recv.at[k - 1],
                (p, c),
            )

    def block(n):
        return block_high[n], block_low[n]

    @pl.when(q == 0)
    def _():
        load_inverse(0).wait()
        pieces[0, :, 0:SLC] = dot3(right[...], split(inv[0]), 1)
        pl.semaphore_wait(barrier, 1)
        push(pieces.at[0], pieces.at[0], first_send, piece_recv.at[0], (p, 1))

    @pl.when(q == 1)
    def _():
        load_panel(0).wait()
        split_block(0, lambda j: panel_tile(0, j))
        pl.semaphore_wait(barrier, len(CHAIN) + 1)
        wait(pieces.at[0], piece_recv.at[0])
        base[...] = own * right[...] - dot3(pieces[0, :, 0:SLC], block(0), 0)
        send_base(1)
        push(pieces.at[0], pieces.at[0], first_send, piece_recv.at[0], (p, 3))

    def send_block(k):
        for n, c in enumerate(CHAIN):
            push(
                flat.at[pl.ds((k - 1) * SLC * TILES, SLC * TILES)],
                rep_flat.at[k - 2],
                rep_send.at[n],
                rep_recv.at[k - 2],
                (p, c),
            )

    @pl.when(q == 2)
    def _():
        load_panel(1).wait()
        pl.semaphore_wait(barrier, len(CHAIN) + 1)
        send_block(2)
        load_panel(0).wait()
        split_block(0, lambda j: panel_tile(0, j))
        wait(pieces.at[0], piece_recv.at[0])
        base[...] = own * right[...] - dot3(pieces[0, :, 0:SLC], block(0), 0)
        send_base(2)
        for n in range(len(CHAIN)):
            wait(rep_flat.at[0], rep_send.at[n])
        pl.semaphore_signal(rep_turn, inc=1, device_id=(p, 3), device_id_type=MESH)

    @pl.when(q == 3)
    def _():
        for k in range(2):
            load_panel(k).wait()
            split_block(k, lambda j: panel_tile(k, j))
        load_panel(2).wait()
        pl.semaphore_wait(barrier, COLS - 3)
        wait(pieces.at[0], piece_recv.at[0])
        push(pieces.at[0], pieces.at[0], first_send, piece_recv.at[0], (p, 2))

        def spread_first(i, _):
            push(pieces.at[0], pieces.at[0], piece_send.at[0], piece_recv.at[0], (p, i))
            return 0

        lax.fori_loop(4, COLS, spread_first, 0)
        base[...] = own * right[...] - dot3(pieces[0, :, 0:SLC], block(0), 0)
        pl.semaphore_wait(rep_turn, 1)
        send_block(3)

    @pl.when(is_chain)
    def _():
        pl.semaphore_wait(barrier, ROWS - 1 + COLS - 1)

    @pl.when((q > 3) & jnp.logical_not(is_chain))
    def _():
        pl.semaphore_wait(barrier, ROWS - 1)

    lane = lax.broadcasted_iota(jnp.int32, (SLC, 128), 1)

    def cut_block(k, _):
        for n in range(ROWS):
            tile, shift = (SLC * n) // 128, (SLC * n) % 128
            value = panel_tile(k, tile)
            if shift:
                value = pltpu.roll(value, 128 - shift, 1)
                if shift > 128 - SLC:
                    after = pltpu.roll(panel_tile(k, tile + 1), 128 - shift, 1)
                    value = jnp.where(lane < 128 - shift, value, after)
            at = slice(128 * n, 128 * (n + 1))
            cut_high[k, :, at], cut_low[k, :, at] = split(value)
        return 0

    for k in range(STEPS):
        ready = {0: (1, 2, 3), 1: (2, 3), 2: (3,), 3: ()}[k]
        pending = q >= 0
        for c in ready:
            pending = pending & (q != c)

        @pl.when(pending)
        def _():
            load_panel(k).wait()

    lax.fori_loop(0, STEPS, cut_block, 0)

    def add_piece(k):
        piece = pieces[k, :, 0:SLC]
        for n in range(0, ROWS, 2):
            at = slice(128 * n, 128 * (n + 2))
            term = dot3(piece, (cut_high[k, :, at], cut_low[k, :, at]), 0)
            for h in range(2):
                value = term[:, 128 * h : 128 * (h + 1)]
                if k == 0:
                    acc[n + h] = value
                else:
                    acc[n + h] += value

    def far_first(i):
        return lax.rem(p + 8 + (1 - 2 * lax.rem(i, 2)) * lax.div(i + 1, 2), ROWS)

    @pl.when(is_chain)
    def _():
        rows = pl.ds(pl.multiple_of(PART * g, PART), PART)
        my_cut = pl.ds(pl.multiple_of(CUT * lax.rem(p, 4), 128), CUT)

        def spread(k):
            def send(i, _):
                push(
                    mine.at[k],
                    pieces.at[k, rows],
                    piece_send.at[k],
                    piece_recv.at[k],
                    (p, lax.rem(q + i, COLS)),
                )
                return 0

            lax.fori_loop(1, COLS, send, 0)

        for k in range(1, STEPS):
            load_inverse(k).wait()
            inv_high[k], inv_low[k] = split(inv[k])

        for k in range(1, STEPS):
            wait(base_in.at[k - 1], base_recv.at[k - 1])
            if k == 1:
                rs_out[0] = base_in[0]
            else:
                rs_out[k - 1] = base_in[k - 1] - dot3(mine[k - 1, :, 0:SLC], block(k - 2), 0)

            def scatter(i, _):
                to = far_first(i)
                part = pl.ds(pl.multiple_of(CUT * lax.rem(to, 4), 128), CUT)
                slot = lax.rem(p - to + ROWS, ROWS) - 1
                push(
                    rs_out.at[k - 1, :, part],
                    rs_in.at[k - 1, slot],
                    rs_send.at[k - 1],
                    rs_recv.at[k - 1],
                    (to, q),
                )
                return 0

            lax.fori_loop(0, ROWS - 1, scatter, 0)
            if k == 1:
                wait(pieces.at[0], piece_recv.at[0])
            else:
                spread(k - 1)
                wait(pieces.at[k - 1, pl.ds(0, RHS - PART)], piece_recv.at[k - 1])
                pieces[k - 1, rows, :] = mine[k - 1]
            add_piece(k - 1)

            wait(rs_in.at[k - 1], rs_recv.at[k - 1])
            total = rs_out[k - 1, :, my_cut]
            for n in range(ROWS - 1):
                total = total + rs_in[k - 1, n]
            residue[k - 1, :, my_cut] = total
            for d in (2, -1, 1):
                push(
                    residue.at[k - 1, :, my_cut],
                    residue.at[k - 1, :, my_cut],
                    ag_send.at[k - 1],
                    ag_recv.at[k - 1],
                    (lax.rem(p - d + ROWS, ROWS), q),
                )
            if k < STEPS - 1:
                wait(rep_flat.at[k - 1], rep_recv.at[k - 1])
                split_block(k - 1, lambda j: rep_flat[k - 1, pl.ds(j, SLC, stride=TILES), :])
            wait(residue.at[k - 1, :, pl.ds(0, 3 * CUT)], ag_recv.at[k - 1])
            mine[k, :, 0:SLC] = dot3(residue[k - 1], (inv_high[k], inv_low[k]), 1)
            mine[k, :, SLC:] = jnp.zeros((PART, 128 - SLC), F32)

        last = STEPS - 1
        spread(last)
        wait(pieces.at[last, pl.ds(0, RHS - PART)], piece_recv.at[last])
        pieces[last, rows, :] = mine[last]

    @pl.when(jnp.logical_not(is_chain))
    def _():
        @pl.when(q > 3)
        def _():
            wait(pieces.at[0], piece_recv.at[0])

        add_piece(0)
        wait(pieces.at[1], piece_recv.at[1])

        @pl.when(q == 3)
        def _():
            base[...] = base[...] - dot3(pieces[1, :, 0:SLC], block(1), 0)
            send_base(3)

        add_piece(1)
        wait(pieces.at[2], piece_recv.at[2])
        add_piece(2)
        wait(pieces.at[3], piece_recv.at[3])

    add_piece(STEPS - 1)

    wide = lax.broadcasted_iota(jnp.int32, (8, 128), 1)
    for slot, d in enumerate(ORDER):
        n = lax.rem(p + d, ROWS)
        rest = acc[n, RHS - 8 : RHS, :]
        for a in range(3):
            beside = pltpu.roll(rest, SLC - 32 * a, 1)
            packed[slot, 8 * a : 8 * (a + 1), :] = jnp.where(wide < SLC, acc[n, 8 * a : 8 * (a + 1), :], beside)
        packed[slot, 24 : RHS - 8, :] = acc[n, 24 : RHS - 8, :]
        if slot in (3, 6):
            part = pl.ds(0, 4) if slot == 3 else pl.ds(4, 3)
            to = 1 if slot == 3 else ROWS - 1
            push(packed.at[part], near_in.at[part], near_send, near_recv, (lax.rem(p + to, ROWS), q))

    def finish(slot):
        push(
            packed.at[slot],
            far_in.at[slot - 7],
            far_send,
            far_recv,
            (lax.rem(p + ORDER[slot], ROWS), q),
        )

    finish(14)
    solved_ref[...] = pieces[:, :, 0:SLC]

    tile = lax.div(3 * p, 4)
    shift = 32 * lax.rem(3 * p, 4)
    here = right[:, pl.ds(pl.multiple_of(128 * tile, 128), 128)]
    after = right[:, pl.ds(pl.multiple_of(128 * jnp.minimum(tile + 1, TILES - 1), 128), 128)]
    turn = lax.rem(128 - shift, 128)
    lanes = lax.broadcasted_iota(jnp.int32, (RHS, 128), 1)
    total = jnp.where(lanes < 128 - shift, pltpu.roll(here, turn, 1), pltpu.roll(after, turn, 1))

    wait(near_in, near_recv)
    for slot in (10, 9, 13, 8, 12, 7, 11):
        packed[slot] = packed[slot] + near_in[slot - 7]
        finish(slot)
    term = packed[15]
    wait(far_in, far_recv)
    for n in range(8):
        term = term + far_in[n]
    updated_ref[0 : RHS - 8, :] = (total[0 : RHS - 8, :] - term)[:, 0:SLC]
    last = jnp.where(wide < 32, pltpu.roll(term[0:8, :], 32, 1), pltpu.roll(term[8:16, :], 64, 1))
    last = jnp.where(wide < 64, last, pltpu.roll(term[16:24, :], SLC, 1))
    updated_ref[RHS - 8 : RHS, :] = (total[RHS - 8 : RHS, :] - last)[:, 0:SLC]

    wait(near_in, near_send)
    wait(far_in, far_send)

    @pl.when((q == 0) | (q == 1) | (q == 3))
    def _():
        wait(pieces.at[0], first_send)

    @pl.when((q >= 1) & (q <= 3))
    def _():
        wait(base, base_send)

    @pl.when(q == 3)
    def _():
        wait(flat.at[pl.ds(0, (COLS - 4) * RHS)], piece_send.at[0])
        for n in range(len(CHAIN)):
            wait(rep_flat.at[0], rep_send.at[n])

    @pl.when(is_chain)
    def _():
        for k in range(1, STEPS):
            wait(rs_in.at[k - 1], rs_send.at[k - 1])
            wait(residue.at[k - 1, :, pl.ds(0, 3 * CUT)], ag_send.at[k - 1])
            wait(flat.at[pl.ds(0, (COLS - 1) * PART)], piece_send.at[k])


def body(panel, inverse_blocks, right_side):
    hbm = pl.BlockSpec(memory_space=pl.ANY)
    vmem = pl.BlockSpec(memory_space=pltpu.VMEM)
    dma = pltpu.SemaphoreType.DMA
    solved, updated = pl.pallas_call(
        kernel,
        out_shape=(
            jax.ShapeDtypeStruct((STEPS, RHS, SLC), F32),
            jax.ShapeDtypeStruct((RHS, SLC), F32),
        ),
        in_specs=[hbm, hbm, hbm],
        out_specs=(vmem, vmem),
        scratch_shapes=[
            pltpu.VMEM((STEPS * SLC * TILES, 128), F32),
            pltpu.VMEM((STEPS, SLC, ROWS * 128), BF16),
            pltpu.VMEM((STEPS, SLC, ROWS * 128), BF16),
            pltpu.VMEM((2, SLC * TILES, 128), F32),
            pltpu.VMEM((2, SLC, BLK), BF16),
            pltpu.VMEM((2, SLC, BLK), BF16),
            pltpu.VMEM((STEPS, SLC, BLK), F32),
            pltpu.VMEM((STEPS, SLC, BLK), BF16),
            pltpu.VMEM((STEPS, SLC, BLK), BF16),
            pltpu.VMEM((RHS * TILES, 128), F32),
            pltpu.VMEM((RHS, BLK), F32),
            pltpu.VMEM((STEPS, RHS, 128), F32),
            pltpu.VMEM((RHS, BLK), F32),
            pltpu.VMEM((3, PART, BLK), F32),
            pltpu.VMEM((3, PART, BLK), F32),
            pltpu.VMEM((3, ROWS - 1, PART, CUT), F32),
            pltpu.VMEM((3, PART, BLK), F32),
            pltpu.VMEM((STEPS, PART, 128), F32),
            pltpu.VMEM((ROWS, RHS, 128), F32),
            pltpu.VMEM((ROWS, RHS - 8, 128), F32),
            pltpu.VMEM((7, RHS - 8, 128), F32),
            pltpu.VMEM((8, RHS - 8, 128), F32),
            dma((STEPS,)),
            dma((STEPS,)),
            dma,
            dma((len(CHAIN),)),
            dma((2,)),
            pltpu.SemaphoreType.REGULAR,
            dma,
            dma((STEPS,)),
            dma((STEPS,)),
            dma,
            dma((3,)),
            dma((3,)),
            dma((3,)),
            dma((3,)),
            dma((3,)),
            dma,
            dma,
            dma,
            dma,
        ],
        compiler_params=pltpu.CompilerParams(collective_id=0, has_side_effects=True),
        name="solve",
    )(
        panel.reshape(STEPS * SLC * TILES, 128),
        inverse_blocks,
        right_side.reshape(RHS * TILES, 128),
    )
    return jnp.transpose(solved, (1, 0, 2)), updated.reshape(RHS, 1, 1, SLC)


def solution(mesh):
    placed = (P(None, "row", None, "col", None), P(None, "row", None), P(None, None, "col", None))
    return jax.shard_map(
        body,
        mesh=mesh,
        in_specs=placed,
        out_specs=(P(None, None, "row"), P(None, None, "col", "row")),
        check_vma=False,
    )
```

time: 97.7 us -> 83.4 us (0.85)
  Pallas kernels: 93.4 us -> 79.3 us
    pallas_call x1, Pallas kernels: 93.4 us -> 79.3 us  [body(): pl.pallas_call(kernel, out_shape=(jax.ShapeDtypeStruct((STEPS, RHS, SLC),...]
where the time goes in v2:
time: 83.4 us; the launch traced here: 82.9 us
  Pallas kernels  79.3 us (95%)
  local copies, waits for them, and re-layouts  2.92 us (4%)
    pallas_call x1, Pallas kernels, body(): pl.pallas_call(kernel, out_shape=(jax.ShapeDtypeStruct((STEPS, RHS, SLC),...  79.3 us
    unnamed x2, local copies, waits for them, and re-layouts  2.92 us

profile of v2, /device:TPU:6, one launch (start us, length us, event | category | flops | bytes accessed | tf_op | source)
XLA Modules:
  0.0 82.9 jit_solution(5869633835817287248)
XLA Ops:
  0.6 79.3 %solve.1 = (f32[4,48,96]{2,1,0:T(8,128)}, f32[48,96]{1,0:T(8,128)}) custom-call(f32[4608,128]{1,0:T(8,128)} %bitcast.6, f32[4,96,1536]{2,1,0:T(8,128)} %inverse_ref.1, f32[576,128]{1,0:T(8,128)} %bitcast.7), custom_call_target="tpu_custom_call" | custom-call | tf_op jit(solution)/shard_map/solve/pallas_call | solution.py:461
  79.9 1.6 %copy.5 = f32[48,4,96]{2,1,0:T(4,128)} copy(f32[48,4,96]{2,0,1:T(8,128)} %bitcast.8) | data formatting | bytes 147456
  81.5 1.3 %copy.8 = f32[48,1,1,96]{3,2,1,0:T(1,128)} copy(f32[48,1,1,96]{3,2,1,0:T(1,128)} %bitcast.9) | data formatting | bytes 36864

commit v3 on v2

--- a/solution.py
+++ b/solution.py
@@ -11,10 +11,17 @@
 ROWS, COLS = 16, 32
 STEPS, RHS, BLK, SLC = 4, 48, 1536, 96
 TILES = BLK // 128
-CHAIN = (4, 6, 8, 10, 24, 26)
+CHAIN = (4, 6, 8, 10, 12, 14, 16, 18, 24, 26, 28, 30)
+RELAYS = {5: (4, 6, 14, 30), 11: (10, 8, 12, 18), 27: (26, 24, 28, 16)}
+THIRD = SLC * BLK // 128 // 3
 PART = RHS // len(CHAIN)
 CUT = BLK // 4
 ORDER = (2, 4, 6, 8, 14, 12, 10, 1, 3, 5, 7, 15, 13, 11, 9, 0)
+AROUND = sorted(
+    [(x, y, c) for x in range(4) for y in range(4) for c in range(2) if x or y or c],
+    key=lambda d: (-min(d[0], 4 - d[0]) - min(d[1], 4 - d[1]), d),
+)
+TAIL = RHS - RHS // 4
 
 
 def split(value):
@@ -24,9 +31,11 @@
 
 def dot3(left, right, axis):
     rows = left.shape[0]
-    high, low = split(left)
+    high = left.astype(BF16)
+    wide = high.astype(F32)
+    stacked = jnp.concatenate([wide, left - wide], 0).astype(BF16)
     dims = (((1,), (axis,)), ((), ()))
-    both = lax.dot_general(jnp.concatenate([high, low], 0), right[0], dims, preferred_element_type=F32)
+    both = lax.dot_general(stacked, right[0], dims, preferred_element_type=F32)
     rest = lax.dot_general(high, right[1], dims, preferred_element_type=F32)
     return both[:rows] + (both[rows:] + rest)
 
@@ -49,7 +58,9 @@
     right_flat,
     right,
     pieces,
+    parts,
     base,
+    base_out,
     base_in,
     rs_out,
     rs_in,
@@ -65,6 +76,7 @@
     rep_send,
     rep_recv,
     rep_turn,
+    relay_send,
     first_send,
     piece_send,
     piece_recv,
@@ -81,11 +93,9 @@
 ):
     p = lax.axis_index("row")
     q = lax.axis_index("col")
-    is_chain = q == CHAIN[0]
-    g = jnp.int32(0)
-    for n, c in enumerate(CHAIN):
-        is_chain = is_chain | (q == c)
-        g = g + jnp.where(q == c, n, 0)
+    is_chain = (lax.rem(q, 2) == 0) & (q > 3) & (q != 20) & (q != 22)
+    g = jnp.where(q < 20, lax.div(q - 4, 2), lax.div(q - 8, 2))
+    is_relay = (q == 5) | (q == 11) | (q == 27)
 
     def wait(ref, sem):
         pltpu.make_async_copy(ref, ref, sem).wait()
@@ -124,7 +134,16 @@
     @pl.when(is_chain | (q == 3))
     def _():
         hello(p, 1)
+
+    @pl.when(is_chain | is_relay | (q == 3))
+    def _():
         hello(p, 2)
+
+    for r, group in RELAYS.items():
+
+        @pl.when((q == group[0]) | (q == group[1]) | (q == group[2]) | (q == group[3]))
+        def _():
+            hello(p, r)
 
     for c in CHAIN:
 
@@ -165,8 +184,9 @@
 
     def send_base(k):
         for n, c in enumerate(CHAIN):
+            base_out[n] = base[PART * n : PART * (n + 1), :]
             push(
-                base.at[pl.ds(PART * n, PART)],
+                base_out.at[n],
                 base_in.at[k - 1],
                 base_send,
                 base_recv.at[k - 1],
@@ -194,27 +214,42 @@
         push(pieces.at[0], pieces.at[0], first_send, piece_recv.at[0], (p, 3))
 
     def send_block(k):
-        for n, c in enumerate(CHAIN):
-            push(
-                flat.at[pl.ds((k - 1) * SLC * TILES, SLC * TILES)],
-                rep_flat.at[k - 2],
-                rep_send.at[n],
-                rep_recv.at[k - 2],
-                (p, c),
-            )
+        for n in range(3):
+            for r in RELAYS:
+                push(
+                    flat.at[pl.ds((k - 1) * SLC * TILES + n * THIRD, THIRD)],
+                    rep_flat.at[k - 2, pl.ds(n * THIRD, THIRD)],
+                    rep_send,
+                    rep_recv.at[k - 2, n],
+                    (p, r),
+                )
+
+    def hand_on(m):
+        for n in range(3):
+            part = rep_flat.at[m, pl.ds(n * THIRD, THIRD)]
+            wait(part, rep_recv.at[m, n])
+            for r, group in RELAYS.items():
+
+                @pl.when(q == r)
+                def _():
+                    for c in group:
+                        push(part, part, relay_send.at[m], rep_recv.at[m, n], (p, c))
+
+    def wait_block(m):
+        for n in range(3):
+            wait(rep_flat.at[m, pl.ds(n * THIRD, THIRD)], rep_recv.at[m, n])
 
     @pl.when(q == 2)
     def _():
         load_panel(1).wait()
-        pl.semaphore_wait(barrier, len(CHAIN) + 1)
+        pl.semaphore_wait(barrier, len(CHAIN) + len(RELAYS) + 1)
         send_block(2)
         load_panel(0).wait()
         split_block(0, lambda j: panel_tile(0, j))
         wait(pieces.at[0], piece_recv.at[0])
         base[...] = own * right[...] - dot3(pieces[0, :, 0:SLC], block(0), 0)
         send_base(2)
-        for n in range(len(CHAIN)):
-            wait(rep_flat.at[0], rep_send.at[n])
+        wait(flat.at[pl.ds(0, 9 * THIRD)], rep_send)
         pl.semaphore_signal(rep_turn, inc=1, device_id=(p, 3), device_id_type=MESH)
 
     @pl.when(q == 3)
@@ -240,9 +275,14 @@
     def _():
         pl.semaphore_wait(barrier, ROWS - 1 + COLS - 1)
 
-    @pl.when((q > 3) & jnp.logical_not(is_chain))
+    @pl.when((q > 3) & jnp.logical_not(is_chain | is_relay))
     def _():
         pl.semaphore_wait(barrier, ROWS - 1)
+
+    @pl.when(is_relay)
+    def _():
+        pl.semaphore_wait(barrier, ROWS - 1 + 4)
+        hand_on(0)
 
     lane = lax.broadcasted_iota(jnp.int32, (SLC, 128), 1)
 
@@ -272,6 +312,9 @@
     lax.fori_loop(0, STEPS, cut_block, 0)
 
     def add_piece(k):
+        if k:
+            for n in range(len(CHAIN)):
+                pieces[k, PART * n : PART * (n + 1), :] = parts[k - 1, n]
         piece = pieces[k, :, 0:SLC]
         for n in range(0, ROWS, 2):
             at = slice(128 * n, 128 * (n + 2))
@@ -288,21 +331,21 @@
 
     @pl.when(is_chain)
     def _():
-        rows = pl.ds(pl.multiple_of(PART * g, PART), PART)
         my_cut = pl.ds(pl.multiple_of(CUT * lax.rem(p, 4), 128), CUT)
+
+        def spread_to(k, to):
+            push(mine.at[k], parts.at[k - 1, g], piece_send.at[k], piece_recv.at[k], (p, to))
 
         def spread(k):
             def send(i, _):
-                push(
-                    mine.at[k],
-                    pieces.at[k, rows],
-                    piece_send.at[k],
-                    piece_recv.at[k],
-                    (p, lax.rem(q + i, COLS)),
-                )
+                spread_to(k, lax.rem(q + i, COLS))
                 return 0
 
             lax.fori_loop(1, COLS, send, 0)
+
+        def others(k):
+            wait(parts.at[k - 1, pl.ds(0, len(CHAIN) - 1)], piece_recv.at[k])
+            parts[k - 1, g] = mine[k]
 
         for k in range(1, STEPS):
             load_inverse(k).wait()
@@ -333,8 +376,7 @@
                 wait(pieces.at[0], piece_recv.at[0])
             else:
                 spread(k - 1)
-                wait(pieces.at[k - 1, pl.ds(0, RHS - PART)], piece_recv.at[k - 1])
-                pieces[k - 1, rows, :] = mine[k - 1]
+                others(k - 1)
             add_piece(k - 1)
 
             wait(rs_in.at[k - 1], rs_recv.at[k - 1])
@@ -351,16 +393,18 @@
                     (lax.rem(p - d + ROWS, ROWS), q),
                 )
             if k < STEPS - 1:
-                wait(rep_flat.at[k - 1], rep_recv.at[k - 1])
+                wait_block(k - 1)
                 split_block(k - 1, lambda j: rep_flat[k - 1, pl.ds(j, SLC, stride=TILES), :])
             wait(residue.at[k - 1, :, pl.ds(0, 3 * CUT)], ag_recv.at[k - 1])
             mine[k, :, 0:SLC] = dot3(residue[k - 1], (inv_high[k], inv_low[k]), 1)
             mine[k, :, SLC:] = jnp.zeros((PART, 128 - SLC), F32)
 
         last = STEPS - 1
-        spread(last)
-        wait(pieces.at[last, pl.ds(0, RHS - PART)], piece_recv.at[last])
-        pieces[last, rows, :] = mine[last]
+        x, y, core = lax.div(q, 8), lax.rem(lax.div(q, 2), 4), lax.rem(q, 2)
+        for dx, dy, dc in AROUND:
+            to = lax.rem(x + dx, 4) * 8 + lax.rem(y + dy, 4) * 2 + lax.rem(core + dc, 2)
+            spread_to(last, to)
+        others(last)
 
     @pl.when(jnp.logical_not(is_chain))
     def _():
@@ -369,28 +413,32 @@
             wait(pieces.at[0], piece_recv.at[0])
 
         add_piece(0)
-        wait(pieces.at[1], piece_recv.at[1])
+
+        @pl.when(is_relay)
+        def _():
+            hand_on(1)
+
+        wait(parts.at[0], piece_recv.at[1])
+        add_piece(1)
 
         @pl.when(q == 3)
         def _():
             base[...] = base[...] - dot3(pieces[1, :, 0:SLC], block(1), 0)
             send_base(3)
 
-        add_piece(1)
-        wait(pieces.at[2], piece_recv.at[2])
+        wait(parts.at[1], piece_recv.at[2])
         add_piece(2)
-        wait(pieces.at[3], piece_recv.at[3])
+        wait(parts.at[2], piece_recv.at[3])
 
     add_piece(STEPS - 1)
 
-    wide = lax.broadcasted_iota(jnp.int32, (8, 128), 1)
+    wide = lax.broadcasted_iota(jnp.int32, (RHS // 4, 128), 1)
     for slot, d in enumerate(ORDER):
         n = lax.rem(p + d, ROWS)
-        rest = acc[n, RHS - 8 : RHS, :]
+        rest = acc[n, TAIL:RHS, :]
         for a in range(3):
-            beside = pltpu.roll(rest, SLC - 32 * a, 1)
-            packed[slot, 8 * a : 8 * (a + 1), :] = jnp.where(wide < SLC, acc[n, 8 * a : 8 * (a + 1), :], beside)
-        packed[slot, 24 : RHS - 8, :] = acc[n, 24 : RHS - 8, :]
+            at = slice(RHS // 4 * a, RHS // 4 * (a + 1))
+            packed[slot, at, :] = jnp.where(wide < SLC, acc[n, at, :], pltpu.roll(rest, SLC - 32 * a, 1))
         if slot in (3, 6):
             part = pl.ds(0, 4) if slot == 3 else pl.ds(4, 3)
             to = 1 if slot == 3 else ROWS - 1
@@ -424,10 +472,13 @@
     wait(far_in, far_recv)
     for n in range(8):
         term = term + far_in[n]
-    updated_ref[0 : RHS - 8, :] = (total[0 : RHS - 8, :] - term)[:, 0:SLC]
-    last = jnp.where(wide < 32, pltpu.roll(term[0:8, :], 32, 1), pltpu.roll(term[8:16, :], 64, 1))
-    last = jnp.where(wide < 64, last, pltpu.roll(term[16:24, :], SLC, 1))
-    updated_ref[RHS - 8 : RHS, :] = (total[RHS - 8 : RHS, :] - last)[:, 0:SLC]
+    acc[0] = total
+    acc[1, 0:TAIL, :] = term
+    updated_ref[0:TAIL, :] = (acc[1, 0:TAIL, :] - acc[0, 0:TAIL, :])[:, 0:SLC]
+    last = pltpu.roll(acc[1, RHS // 2 : TAIL, :], SLC, 1)
+    last = jnp.where(wide < 64, pltpu.roll(acc[1, RHS // 4 : RHS // 2, :], 64, 1), last)
+    last = jnp.where(wide < 32, pltpu.roll(acc[1, 0 : RHS // 4, :], 32, 1), last)
+    updated_ref[TAIL:RHS, :] = (last - acc[0, TAIL:RHS, :])[:, 0:SLC]
 
     wait(near_in, near_send)
     wait(far_in, far_send)
@@ -438,13 +489,17 @@
 
     @pl.when((q >= 1) & (q <= 3))
     def _():
-        wait(base, base_send)
+        wait(base_out, base_send)
 
     @pl.when(q == 3)
     def _():
         wait(flat.at[pl.ds(0, (COLS - 4) * RHS)], piece_send.at[0])
-        for n in range(len(CHAIN)):
-            wait(rep_flat.at[0], rep_send.at[n])
+        wait(flat.at[pl.ds(0, 9 * THIRD)], rep_send)
+
+    @pl.when(is_relay)
+    def _():
+        for m in range(2):
+            wait(flat, relay_send.at[m])
 
     @pl.when(is_chain)
     def _():
@@ -455,14 +510,14 @@
 
 
 def body(panel, inverse_blocks, right_side):
-    hbm = pl.BlockSpec(memory_space=pl.ANY)
+    hbm = pl.BlockSpec(memory_space=pltpu.HBM)
     vmem = pl.BlockSpec(memory_space=pltpu.VMEM)
     dma = pltpu.SemaphoreType.DMA
     solved, updated = pl.pallas_call(
         kernel,
         out_shape=(
-            jax.ShapeDtypeStruct((STEPS, RHS, SLC), F32),
-            jax.ShapeDtypeStruct((RHS, SLC), F32),
+            pltpu.VMEM((STEPS, RHS, SLC), F32),
+            pltpu.VMEM((RHS, SLC), F32),
         ),
         in_specs=[hbm, hbm, hbm],
         out_specs=(vmem, vmem),
@@ -479,22 +534,25 @@
             pltpu.VMEM((RHS * TILES, 128), F32),
             pltpu.VMEM((RHS, BLK), F32),
             pltpu.VMEM((STEPS, RHS, 128), F32),
+            pltpu.VMEM((3, len(CHAIN), PART, 128), F32),
             pltpu.VMEM((RHS, BLK), F32),
+            pltpu.VMEM((len(CHAIN), PART, BLK), F32),
             pltpu.VMEM((3, PART, BLK), F32),
             pltpu.VMEM((3, PART, BLK), F32),
             pltpu.VMEM((3, ROWS - 1, PART, CUT), F32),
             pltpu.VMEM((3, PART, BLK), F32),
             pltpu.VMEM((STEPS, PART, 128), F32),
             pltpu.VMEM((ROWS, RHS, 128), F32),
-            pltpu.VMEM((ROWS, RHS - 8, 128), F32),
-            pltpu.VMEM((7, RHS - 8, 128), F32),
-            pltpu.VMEM((8, RHS - 8, 128), F32),
+            pltpu.VMEM((ROWS, TAIL, 128), F32),
+            pltpu.VMEM((7, TAIL, 128), F32),
+            pltpu.VMEM((8, TAIL, 128), F32),
             dma((STEPS,)),
             dma((STEPS,)),
             dma,
-            dma((len(CHAIN),)),
+            dma,
+            dma((2, 3)),
+            pltpu.SemaphoreType.REGULAR,
             dma((2,)),
-            pltpu.SemaphoreType.REGULAR,
             dma,
             dma((STEPS,)),
             dma((STEPS,)),
@@ -509,14 +567,14 @@
             dma,
             dma,
         ],
-        compiler_params=pltpu.CompilerParams(collective_id=0, has_side_effects=True),
+        compiler_params=pltpu.CompilerParams(collective_id=0, has_side_effects=True, vmem_limit_bytes=61500 * 1024),
         name="solve",
     )(
         panel.reshape(STEPS * SLC * TILES, 128),
         inverse_blocks,
         right_side.reshape(RHS * TILES, 128),
     )
-    return jnp.transpose(solved, (1, 0, 2)), updated.reshape(RHS, 1, 1, SLC)
+    return jnp.transpose(solved, (1, 0, 2)), -updated.reshape(RHS, 1, 1, SLC)
 
 
 def solution(mesh):

time: 83.4 us -> 73.7 us (0.88)
  Pallas kernels: 79.3 us -> 71.4 us
  local copies, waits for them, and re-layouts: 2.92 us -> 0.68 us
    pallas_call x1, Pallas kernels: 79.3 us -> 71.4 us  [body(): pl.pallas_call(kernel, out_shape=(pltpu.VMEM((STEPS, RHS, SLC), F32), plt...]
    unnamed x2 -> x1, local copies, waits for them, and re-layouts: 2.92 us -> 0.68 us
where the time goes in v3:
time: 73.7 us; the launch traced here: 73.4 us
  Pallas kernels  71.4 us (97%)
    pallas_call x1, Pallas kernels, body(): pl.pallas_call(kernel, out_shape=(pltpu.VMEM((STEPS, RHS, SLC), F32), plt...  71.4 us

profile of v3, /device:TPU:6, one launch (start us, length us, event | category | flops | bytes accessed | tf_op | source)
XLA Modules:
  0.0 73.4 jit_solution(2208349290925814273)
XLA Ops:
  0.6 71.4 %solve.1 = (f32[4,48,96]{2,1,0:T(8,128)S(1)}, f32[48,96]{1,0:T(8,128)S(1)}) custom-call(f32[4608,128]{1,0:T(8,128)} %bitcast.7, f32[4,96,1536]{2,1,0:T(8,128)} %inverse_ref.1, f32[576,128]{1,0:T(8,128)} %bitcast.8), custom_call_target="tpu_custom_call" | custom-call | tf_op jit(solution)/shard_map/solve/pallas_call | solution.py:516
  72.1 0.7 copy.5
  72.8 0.6 neg.6

commit v4 on v3

--- a/solution.py
+++ b/solution.py
@@ -16,12 +16,12 @@
 THIRD = SLC * BLK // 128 // 3
 PART = RHS // len(CHAIN)
 CUT = BLK // 4
-ORDER = (2, 4, 6, 8, 14, 12, 10, 1, 3, 5, 7, 15, 13, 11, 9, 0)
 AROUND = sorted(
     [(x, y, c) for x in range(4) for y in range(4) for c in range(2) if x or y or c],
     key=lambda d: (-min(d[0], 4 - d[0]) - min(d[1], 4 - d[1]), d),
 )
 TAIL = RHS - RHS // 4
+HALF = ROWS // 2 * 128
 
 
 def split(value):
@@ -59,6 +59,13 @@
     right,
     pieces,
     parts,
+    last_parts,
+    last_mine,
+    give,
+    taken,
+    inv_other,
+    last_high,
+    last_low,
     base,
     base_out,
     base_in,
@@ -68,6 +75,7 @@
     mine,
     acc,
     packed,
+    near_out,
     near_in,
     far_in,
     panel_sem,
@@ -86,6 +94,10 @@
     rs_recv,
     ag_send,
     ag_recv,
+    give_send,
+    give_recv,
+    other_send,
+    other_recv,
     near_send,
     near_recv,
     far_send,
@@ -96,6 +108,7 @@
     is_chain = (lax.rem(q, 2) == 0) & (q > 3) & (q != 20) & (q != 22)
     g = jnp.where(q < 20, lax.div(q - 4, 2), lax.div(q - 8, 2))
     is_relay = (q == 5) | (q == 11) | (q == 27)
+    pair = p + 1 - 2 * lax.rem(p, 2)
 
     def wait(ref, sem):
         pltpu.make_async_copy(ref, ref, sem).wait()
@@ -154,6 +167,10 @@
     @pl.when((q == 2) | (q > 3))
     def _():
         hello(p, 3)
+
+    @pl.when(q == 3)
+    def _():
+        hello(pair, 3)
 
     @pl.when(q > 3)
     def _():
@@ -258,7 +275,7 @@
             load_panel(k).wait()
             split_block(k, lambda j: panel_tile(k, j))
         load_panel(2).wait()
-        pl.semaphore_wait(barrier, COLS - 3)
+        pl.semaphore_wait(barrier, COLS - 3 + 1)
         wait(pieces.at[0], piece_recv.at[0])
         push(pieces.at[0], pieces.at[0], first_send, piece_recv.at[0], (p, 2))
 
@@ -286,18 +303,32 @@
 
     lane = lax.broadcasted_iota(jnp.int32, (SLC, 128), 1)
 
+    def cut_tile(k, slot):
+        n = lax.rem((p if slot < ROWS // 2 else pair) + 2 * slot, ROWS)
+        tile, shift = lax.div(3 * n, 4), 32 * lax.rem(3 * n, 4)
+        turn = lax.rem(128 - shift, 128)
+        value = pltpu.roll(panel_tile(k, tile), turn, 1)
+        after = pltpu.roll(panel_tile(k, jnp.minimum(tile + 1, TILES - 1)), turn, 1)
+        return jnp.where(lane < 128 - shift, value, after)
+
     def cut_block(k, _):
         for n in range(ROWS):
-            tile, shift = (SLC * n) // 128, (SLC * n) % 128
-            value = panel_tile(k, tile)
-            if shift:
-                value = pltpu.roll(value, 128 - shift, 1)
-                if shift > 128 - SLC:
-                    after = pltpu.roll(panel_tile(k, tile + 1), 128 - shift, 1)
-                    value = jnp.where(lane < 128 - shift, value, after)
             at = slice(128 * n, 128 * (n + 1))
-            cut_high[k, :, at], cut_low[k, :, at] = split(value)
+            cut_high[k, :, at], cut_low[k, :, at] = split(cut_tile(k, n))
         return 0
+
+    def cut_last():
+        for n in range(ROWS // 2):
+            at = slice(128 * n, 128 * (n + 1))
+            cut_high[STEPS - 1, :, at], cut_low[STEPS - 1, :, at] = split(cut_tile(STEPS - 1, n))
+            give[:, at] = cut_tile(STEPS - 1, ROWS // 2 + n)
+
+    def exchange_last():
+        push(give, taken, give_send, give_recv, (pair, q))
+
+    def take_last():
+        wait(taken, give_recv)
+        cut_high[STEPS - 1, :, HALF:], cut_low[STEPS - 1, :, HALF:] = split(taken[...])
 
     for k in range(STEPS):
         ready = {0: (1, 2, 3), 1: (2, 3), 2: (3,), 3: ()}[k]
@@ -309,7 +340,13 @@
         def _():
             load_panel(k).wait()
 
-    lax.fori_loop(0, STEPS, cut_block, 0)
+    cut_last()
+
+    @pl.when((q > 2) & jnp.logical_not(is_chain))
+    def _():
+        exchange_last()
+
+    lax.fori_loop(0, STEPS - 1, cut_block, 0)
 
     def add_piece(k):
         if k:
@@ -326,6 +363,23 @@
                 else:
                     acc[n + h] += value
 
+    wide = lax.broadcasted_iota(jnp.int32, (RHS // 4, 128), 1)
+
+    def pack(slot, put):
+        rest = acc[slot, TAIL:RHS, :]
+        for a in range(3):
+            at = slice(RHS // 4 * a, RHS // 4 * (a + 1))
+            put(at, jnp.where(wide < SLC, acc[slot, at, :], pltpu.roll(rest, SLC - 32 * a, 1)))
+
+    def exchange_sums():
+        for n in range(ROWS // 2):
+
+            def put(at, value):
+                near_out[n, at, :] = value
+
+            pack(ROWS // 2 + n, put)
+        push(near_out, near_in, near_send, near_recv, (pair, q))
+
     def far_first(i):
         return lax.rem(p + 8 + (1 - 2 * lax.rem(i, 2)) * lax.div(i + 1, 2), ROWS)
 
@@ -334,7 +388,11 @@
         my_cut = pl.ds(pl.multiple_of(CUT * lax.rem(p, 4), 128), CUT)
 
         def spread_to(k, to):
-            push(mine.at[k], parts.at[k - 1, g], piece_send.at[k], piece_recv.at[k], (p, to))
+            if k == STEPS - 1:
+                src, dst = last_mine, last_parts.at[g]
+            else:
+                src, dst = mine.at[k], parts.at[k - 1, g]
+            push(src, dst, piece_send.at[k], piece_recv.at[k], (p, to))
 
         def spread(k):
             def send(i, _):
@@ -349,7 +407,13 @@
 
         for k in range(1, STEPS):
             load_inverse(k).wait()
-            inv_high[k], inv_low[k] = split(inv[k])
+            if k < STEPS - 1:
+                inv_high[k], inv_low[k] = split(inv[k])
+        none = jnp.zeros((128 - SLC, BLK), BF16)
+        for ref, value in zip((last_high, last_low), split(inv[STEPS - 1])):
+            ref[0:SLC, :] = value
+            ref[SLC:128, :] = none
+            ref[128 + SLC :, :] = none
 
         for k in range(1, STEPS):
             wait(base_in.at[k - 1], base_recv.at[k - 1])
@@ -373,11 +437,20 @@
 
             lax.fori_loop(0, ROWS - 1, scatter, 0)
             if k == 1:
+                exchange_last()
+            if k == 2:
+                push(inv.at[STEPS - 1], inv_other, other_send, other_recv, (pair, q))
+            if k == 1:
                 wait(pieces.at[0], piece_recv.at[0])
             else:
                 spread(k - 1)
                 others(k - 1)
             add_piece(k - 1)
+            if k == STEPS - 1:
+                exchange_sums()
+                wait(inv_other, other_recv)
+                last_high[128 : 128 + SLC, :], last_low[128 : 128 + SLC, :] = split(inv_other[...])
+                take_last()
 
             wait(rs_in.at[k - 1], rs_recv.at[k - 1])
             total = rs_out[k - 1, :, my_cut]
@@ -396,15 +469,21 @@
                 wait_block(k - 1)
                 split_block(k - 1, lambda j: rep_flat[k - 1, pl.ds(j, SLC, stride=TILES), :])
             wait(residue.at[k - 1, :, pl.ds(0, 3 * CUT)], ag_recv.at[k - 1])
-            mine[k, :, 0:SLC] = dot3(residue[k - 1], (inv_high[k], inv_low[k]), 1)
-            mine[k, :, SLC:] = jnp.zeros((PART, 128 - SLC), F32)
+            if k < STEPS - 1:
+                mine[k, :, 0:SLC] = dot3(residue[k - 1], (inv_high[k], inv_low[k]), 1)
+                mine[k, :, SLC:] = jnp.zeros((PART, 128 - SLC), F32)
+            else:
+                both = dot3(residue[k - 1], (last_high[...], last_low[...]), 1)
+                last_mine[0] = both[:, :128]
+                last_mine[1] = both[:, 128:]
 
         last = STEPS - 1
         x, y, core = lax.div(q, 8), lax.rem(lax.div(q, 2), 4), lax.rem(q, 2)
         for dx, dy, dc in AROUND:
             to = lax.rem(x + dx, 4) * 8 + lax.rem(y + dy, 4) * 2 + lax.rem(core + dc, 2)
             spread_to(last, to)
-        others(last)
+        wait(last_parts.at[pl.ds(0, len(CHAIN) - 1)], piece_recv.at[last])
+        last_parts[g] = last_mine[...]
 
     @pl.when(jnp.logical_not(is_chain))
     def _():
@@ -428,33 +507,45 @@
 
         wait(parts.at[1], piece_recv.at[2])
         add_piece(2)
-        wait(parts.at[2], piece_recv.at[3])
-
-    add_piece(STEPS - 1)
-
-    wide = lax.broadcasted_iota(jnp.int32, (RHS // 4, 128), 1)
-    for slot, d in enumerate(ORDER):
-        n = lax.rem(p + d, ROWS)
-        rest = acc[n, TAIL:RHS, :]
-        for a in range(3):
-            at = slice(RHS // 4 * a, RHS // 4 * (a + 1))
-            packed[slot, at, :] = jnp.where(wide < SLC, acc[n, at, :], pltpu.roll(rest, SLC - 32 * a, 1))
-        if slot in (3, 6):
-            part = pl.ds(0, 4) if slot == 3 else pl.ds(4, 3)
-            to = 1 if slot == 3 else ROWS - 1
-            push(packed.at[part], near_in.at[part], near_send, near_recv, (lax.rem(p + to, ROWS), q))
-
-    def finish(slot):
-        push(
-            packed.at[slot],
-            far_in.at[slot - 7],
-            far_send,
-            far_recv,
-            (lax.rem(p + ORDER[slot], ROWS), q),
-        )
-
-    finish(14)
-    solved_ref[...] = pieces[:, :, 0:SLC]
+        exchange_sums()
+
+        @pl.when(q > 2)
+        def _():
+            take_last()
+
+        @pl.when(q < 3)
+        def _():
+            none = jnp.zeros((SLC, HALF), BF16)
+            cut_high[STEPS - 1, :, HALF:] = none
+            cut_low[STEPS - 1, :, HALF:] = none
+
+        wait(last_parts, piece_recv.at[3])
+
+    wait(near_in, near_recv)
+    for n in range(len(CHAIN)):
+        pieces[STEPS - 1, PART * n : PART * (n + 1), :] = last_parts[n, 0]
+        pieces[STEPS, PART * n : PART * (n + 1), :] = last_parts[n, 1]
+    for n in (4, 2, 6, 0):
+        at, to = slice(128 * n, 128 * (n + 2)), slice(HALF + 128 * n, HALF + 128 * (n + 2))
+        term = dot3(pieces[STEPS - 1, :, 0:SLC], (cut_high[STEPS - 1, :, at], cut_low[STEPS - 1, :, at]), 0)
+        term = term + dot3(pieces[STEPS, :, 0:SLC], (cut_high[STEPS - 1, :, to], cut_low[STEPS - 1, :, to]), 0)
+        for slot in (n, n + 1):
+            acc[slot] += term[:, 128 * (slot - n) : 128 * (slot - n + 1)]
+
+            def put(at, value):
+                packed[slot, at, :] = value + near_in[slot, at, :]
+
+            pack(slot, put)
+            if slot:
+                push(
+                    packed.at[slot],
+                    far_in.at[slot - 1],
+                    far_send,
+                    far_recv,
+                    (lax.rem(p + 2 * slot, ROWS), q),
+                )
+
+    solved_ref[...] = pieces[0:STEPS, :, 0:SLC]
 
     tile = lax.div(3 * p, 4)
     shift = 32 * lax.rem(3 * p, 4)
@@ -464,13 +555,9 @@
     lanes = lax.broadcasted_iota(jnp.int32, (RHS, 128), 1)
     total = jnp.where(lanes < 128 - shift, pltpu.roll(here, turn, 1), pltpu.roll(after, turn, 1))
 
-    wait(near_in, near_recv)
-    for slot in (10, 9, 13, 8, 12, 7, 11):
-        packed[slot] = packed[slot] + near_in[slot - 7]
-        finish(slot)
-    term = packed[15]
+    term = packed[0]
     wait(far_in, far_recv)
-    for n in range(8):
+    for n in range(ROWS // 2 - 1):
         term = term + far_in[n]
     acc[0] = total
     acc[1, 0:TAIL, :] = term
@@ -480,8 +567,12 @@
     last = jnp.where(wide < 32, pltpu.roll(acc[1, 0 : RHS // 4, :], 32, 1), last)
     updated_ref[TAIL:RHS, :] = (last - acc[0, TAIL:RHS, :])[:, 0:SLC]
 
-    wait(near_in, near_send)
+    wait(near_out, near_send)
     wait(far_in, far_send)
+
+    @pl.when(q > 2)
+    def _():
+        wait(give, give_send)
 
     @pl.when((q == 0) | (q == 1) | (q == 3))
     def _():
@@ -506,7 +597,8 @@
         for k in range(1, STEPS):
             wait(rs_in.at[k - 1], rs_send.at[k - 1])
             wait(residue.at[k - 1, :, pl.ds(0, 3 * CUT)], ag_send.at[k - 1])
-            wait(flat.at[pl.ds(0, (COLS - 1) * PART)], piece_send.at[k])
+            wait(flat.at[pl.ds(0, (COLS - 1) * PART * (2 if k == STEPS - 1 else 1))], piece_send.at[k])
+        wait(inv_other, other_send)
 
 
 def body(panel, inverse_blocks, right_side):
@@ -533,8 +625,15 @@
             pltpu.VMEM((STEPS, SLC, BLK), BF16),
             pltpu.VMEM((RHS * TILES, 128), F32),
             pltpu.VMEM((RHS, BLK), F32),
-            pltpu.VMEM((STEPS, RHS, 128), F32),
-            pltpu.VMEM((3, len(CHAIN), PART, 128), F32),
+            pltpu.VMEM((STEPS + 1, RHS, 128), F32),
+            pltpu.VMEM((2, len(CHAIN), PART, 128), F32),
+            pltpu.VMEM((len(CHAIN), 2, PART, 128), F32),
+            pltpu.VMEM((2, PART, 128), F32),
+            pltpu.VMEM((SLC, HALF), F32),
+            pltpu.VMEM((SLC, HALF), F32),
+            pltpu.VMEM((SLC, BLK), F32),
+            pltpu.VMEM((256, BLK), BF16),
+            pltpu.VMEM((256, BLK), BF16),
             pltpu.VMEM((RHS, BLK), F32),
             pltpu.VMEM((len(CHAIN), PART, BLK), F32),
             pltpu.VMEM((3, PART, BLK), F32),
@@ -543,9 +642,10 @@
             pltpu.VMEM((3, PART, BLK), F32),
             pltpu.VMEM((STEPS, PART, 128), F32),
             pltpu.VMEM((ROWS, RHS, 128), F32),
-            pltpu.VMEM((ROWS, TAIL, 128), F32),
-            pltpu.VMEM((7, TAIL, 128), F32),
-            pltpu.VMEM((8, TAIL, 128), F32),
+            pltpu.VMEM((ROWS // 2, TAIL, 128), F32),
+            pltpu.VMEM((ROWS // 2, TAIL, 128), F32),
+            pltpu.VMEM((ROWS // 2, TAIL, 128), F32),
+            pltpu.VMEM((ROWS // 2 - 1, TAIL, 128), F32),
             dma((STEPS,)),
             dma((STEPS,)),
             dma,
@@ -562,6 +662,10 @@
             dma((3,)),
             dma((3,)),
             dma((3,)),
+            dma,
+            dma,
+            dma,
+            dma,
             dma,
             dma,
             dma,

time: 73.7 us -> 73.1 us (level)
  the two profiles are of different devices: /device:TPU:6 before, /device:TPU:35 now
where the time goes in v4:
time: 73.1 us; the launch traced here: 72.9 us
  Pallas kernels  71 us (97%)
    pallas_call x1, Pallas kernels, body(): pl.pallas_call(kernel, out_shape=(pltpu.VMEM((STEPS, RHS, SLC), F32), plt...  71 us

profile of v4, /device:TPU:35, one launch (start us, length us, event | category | flops | bytes accessed | tf_op | source)
XLA Modules:
  0.0 72.9 jit_solution(6130717434635269847)
XLA Ops:
  0.6 71.0 %solve.1 = (f32[4,48,96]{2,1,0:T(8,128)S(1)}, f32[48,96]{1,0:T(8,128)S(1)}) custom-call(f32[4608,128]{1,0:T(8,128)} %bitcast.7, f32[4,96,1536]{2,1,0:T(8,128)} %inverse_ref.1, f32[576,128]{1,0:T(8,128)} %bitcast.8), custom_call_target="tpu_custom_call" | custom-call | tf_op jit(solution)/shard_map/solve/pallas_call | solution.py:608
  71.6 0.7 copy.5
  72.3 0.6 neg.6

commit v5 on v4

--- a/solution.py
+++ b/solution.py
@@ -22,6 +22,13 @@
 )
 TAIL = RHS - RHS // 4
 HALF = ROWS // 2 * 128
+
+
+def hops(first, second):
+    total = 0
+    for a, b in ((first // 8, second // 8), (first // 2 % 4, second // 2 % 4)):
+        total += min(abs(a - b), 4 - abs(a - b))
+    return total
 
 
 def split(value):
@@ -59,6 +66,9 @@
     right,
     pieces,
     parts,
+    end_high,
+    end_low,
+    end_piece,
     last_parts,
     last_mine,
     give,
@@ -108,7 +118,13 @@
     is_chain = (lax.rem(q, 2) == 0) & (q > 3) & (q != 20) & (q != 22)
     g = jnp.where(q < 20, lax.div(q - 4, 2), lax.div(q - 8, 2))
     is_relay = (q == 5) | (q == 11) | (q == 27)
-    pair = p + 1 - 2 * lax.rem(p, 2)
+    is_beside = (lax.rem(q, 2) == 1) & (q > 3) & (q != 21) & (q != 23)
+    side = 2 * lax.rem(p, 2) - 1
+    pair = p - side
+
+    def target(slot):
+        return lax.rem(p + side * slot + ROWS, ROWS)
+
 
     def wait(ref, sem):
         pltpu.make_async_copy(ref, ref, sem).wait()
@@ -148,6 +164,19 @@
     def _():
         hello(p, 1)
 
+    @pl.when(is_chain)
+    def _():
+        def ring(i, _):
+            hello(lax.rem(p + 8 + (1 - 2 * lax.rem(i, 2)) * lax.div(i + 1, 2), ROWS), q)
+            return 0
+
+        lax.fori_loop(0, ROWS - 1, ring, 0)
+        hello(pair, q + 1)
+
+    @pl.when((q > 2) & jnp.logical_not(is_chain))
+    def _():
+        hello(pair, q)
+
     @pl.when(is_chain | is_relay | (q == 3))
     def _():
         hello(p, 2)
@@ -167,18 +196,6 @@
     @pl.when((q == 2) | (q > 3))
     def _():
         hello(p, 3)
-
-    @pl.when(q == 3)
-    def _():
-        hello(pair, 3)
-
-    @pl.when(q > 3)
-    def _():
-        def ring(i, _):
-            hello(lax.rem(p + i, ROWS), q)
-            return 0
-
-        lax.fori_loop(1, ROWS, ring, 0)
 
     @pl.when(is_chain)
     def _():
@@ -200,7 +217,7 @@
     own = jnp.where(p == 0, 1.0, 0.0).astype(F32)
 
     def send_base(k):
-        for n, c in enumerate(CHAIN):
+        for n, c in sorted(enumerate(CHAIN), key=lambda v: -hops(v[1], k)):
             base_out[n] = base[PART * n : PART * (n + 1), :]
             push(
                 base_out.at[n],
@@ -292,19 +309,26 @@
     def _():
         pl.semaphore_wait(barrier, ROWS - 1 + COLS - 1)
 
-    @pl.when((q > 3) & jnp.logical_not(is_chain | is_relay))
-    def _():
-        pl.semaphore_wait(barrier, ROWS - 1)
+    @pl.when((q > 3) & jnp.logical_not(is_chain | is_beside))
+    def _():
+        pl.semaphore_wait(barrier, 1)
+
+    @pl.when(is_beside & jnp.logical_not(is_relay))
+    def _():
+        pl.semaphore_wait(barrier, 2)
 
     @pl.when(is_relay)
     def _():
-        pl.semaphore_wait(barrier, ROWS - 1 + 4)
-        hand_on(0)
+        pl.semaphore_wait(barrier, 2 + 4)
+
+    @pl.when(is_beside)
+    def _():
+        push(inverse_ref.at[STEPS - 1], inv_other, other_send, other_recv, (pair, q - 1))
 
     lane = lax.broadcasted_iota(jnp.int32, (SLC, 128), 1)
 
     def cut_tile(k, slot):
-        n = lax.rem((p if slot < ROWS // 2 else pair) + 2 * slot, ROWS)
+        n = target(slot) if slot < ROWS // 2 else lax.rem(pair - side * (slot - ROWS // 2) + ROWS, ROWS)
         tile, shift = lax.div(3 * n, 4), 32 * lax.rem(3 * n, 4)
         turn = lax.rem(128 - shift, 128)
         value = pltpu.roll(panel_tile(k, tile), turn, 1)
@@ -318,9 +342,13 @@
         return 0
 
     def cut_last():
+        none = jnp.zeros((128 - SLC, HALF), BF16)
+        for ref in (end_high, end_low):
+            ref[SLC:128, :] = none
+            ref[128 + SLC :, :] = none
         for n in range(ROWS // 2):
             at = slice(128 * n, 128 * (n + 1))
-            cut_high[STEPS - 1, :, at], cut_low[STEPS - 1, :, at] = split(cut_tile(STEPS - 1, n))
+            end_high[0:SLC, at], end_low[0:SLC, at] = split(cut_tile(STEPS - 1, n))
             give[:, at] = cut_tile(STEPS - 1, ROWS // 2 + n)
 
     def exchange_last():
@@ -328,7 +356,7 @@
 
     def take_last():
         wait(taken, give_recv)
-        cut_high[STEPS - 1, :, HALF:], cut_low[STEPS - 1, :, HALF:] = split(taken[...])
+        end_high[128 : 128 + SLC, :], end_low[128 : 128 + SLC, :] = split(taken[...])
 
     for k in range(STEPS):
         ready = {0: (1, 2, 3), 1: (2, 3), 2: (3,), 3: ()}[k]
@@ -345,6 +373,10 @@
     @pl.when((q > 2) & jnp.logical_not(is_chain))
     def _():
         exchange_last()
+
+    @pl.when(is_relay)
+    def _():
+        hand_on(0)
 
     lax.fori_loop(0, STEPS - 1, cut_block, 0)
 
@@ -438,16 +470,12 @@
             lax.fori_loop(0, ROWS - 1, scatter, 0)
             if k == 1:
                 exchange_last()
-            if k == 2:
-                push(inv.at[STEPS - 1], inv_other, other_send, other_recv, (pair, q))
             if k == 1:
                 wait(pieces.at[0], piece_recv.at[0])
+                add_piece(0)
             else:
                 spread(k - 1)
-                others(k - 1)
-            add_piece(k - 1)
             if k == STEPS - 1:
-                exchange_sums()
                 wait(inv_other, other_recv)
                 last_high[128 : 128 + SLC, :], last_low[128 : 128 + SLC, :] = split(inv_other[...])
                 take_last()
@@ -465,6 +493,11 @@
                     ag_recv.at[k - 1],
                     (lax.rem(p - d + ROWS, ROWS), q),
                 )
+            if k > 1:
+                others(k - 1)
+                add_piece(k - 1)
+            if k == STEPS - 1:
+                exchange_sums()
             if k < STEPS - 1:
                 wait_block(k - 1)
                 split_block(k - 1, lambda j: rep_flat[k - 1, pl.ds(j, SLC, stride=TILES), :])
@@ -516,20 +549,19 @@
         @pl.when(q < 3)
         def _():
             none = jnp.zeros((SLC, HALF), BF16)
-            cut_high[STEPS - 1, :, HALF:] = none
-            cut_low[STEPS - 1, :, HALF:] = none
+            end_high[128 : 128 + SLC, :] = none
+            end_low[128 : 128 + SLC, :] = none
 
         wait(last_parts, piece_recv.at[3])
 
     wait(near_in, near_recv)
     for n in range(len(CHAIN)):
-        pieces[STEPS - 1, PART * n : PART * (n + 1), :] = last_parts[n, 0]
-        pieces[STEPS, PART * n : PART * (n + 1), :] = last_parts[n, 1]
-    for n in (4, 2, 6, 0):
-        at, to = slice(128 * n, 128 * (n + 2)), slice(HALF + 128 * n, HALF + 128 * (n + 2))
-        term = dot3(pieces[STEPS - 1, :, 0:SLC], (cut_high[STEPS - 1, :, at], cut_low[STEPS - 1, :, at]), 0)
-        term = term + dot3(pieces[STEPS, :, 0:SLC], (cut_high[STEPS - 1, :, to], cut_low[STEPS - 1, :, to]), 0)
-        for slot in (n, n + 1):
+        for h in range(2):
+            end_piece[PART * n : PART * (n + 1), 128 * h : 128 * (h + 1)] = last_parts[n, h]
+    for n in (6, 4, 2, 0):
+        at = slice(128 * n, 128 * (n + 2))
+        term = dot3(end_piece[...], (end_high[:, at], end_low[:, at]), 0)
+        for slot in (n + 1, n):
             acc[slot] += term[:, 128 * (slot - n) : 128 * (slot - n + 1)]
 
             def put(at, value):
@@ -542,10 +574,11 @@
                     far_in.at[slot - 1],
                     far_send,
                     far_recv,
-                    (lax.rem(p + 2 * slot, ROWS), q),
+                    (target(slot), q),
                 )
 
-    solved_ref[...] = pieces[0:STEPS, :, 0:SLC]
+    solved_ref[0 : STEPS - 1] = pieces[:, :, 0:SLC]
+    solved_ref[STEPS - 1] = end_piece[:, 0:SLC]
 
     tile = lax.div(3 * p, 4)
     shift = 32 * lax.rem(3 * p, 4)
@@ -574,6 +607,10 @@
     def _():
         wait(give, give_send)
 
+    @pl.when(is_beside)
+    def _():
+        wait(inv_other, other_send)
+
     @pl.when((q == 0) | (q == 1) | (q == 3))
     def _():
         wait(pieces.at[0], first_send)
@@ -598,7 +635,6 @@
             wait(rs_in.at[k - 1], rs_send.at[k - 1])
             wait(residue.at[k - 1, :, pl.ds(0, 3 * CUT)], ag_send.at[k - 1])
             wait(flat.at[pl.ds(0, (COLS - 1) * PART * (2 if k == STEPS - 1 else 1))], piece_send.at[k])
-        wait(inv_other, other_send)
 
 
 def body(panel, inverse_blocks, right_side):
@@ -615,8 +651,8 @@
         out_specs=(vmem, vmem),
         scratch_shapes=[
             pltpu.VMEM((STEPS * SLC * TILES, 128), F32),
-            pltpu.VMEM((STEPS, SLC, ROWS * 128), BF16),
-            pltpu.VMEM((STEPS, SLC, ROWS * 128), BF16),
+            pltpu.VMEM((STEPS - 1, SLC, ROWS * 128), BF16),
+            pltpu.VMEM((STEPS - 1, SLC, ROWS * 128), BF16),
             pltpu.VMEM((2, SLC * TILES, 128), F32),
             pltpu.VMEM((2, SLC, BLK), BF16),
             pltpu.VMEM((2, SLC, BLK), BF16),
@@ -625,8 +661,11 @@
             pltpu.VMEM((STEPS, SLC, BLK), BF16),
             pltpu.VMEM((RHS * TILES, 128), F32),
             pltpu.VMEM((RHS, BLK), F32),
-            pltpu.VMEM((STEPS + 1, RHS, 128), F32),
+            pltpu.VMEM((STEPS - 1, RHS, 128), F32),
             pltpu.VMEM((2, len(CHAIN), PART, 128), F32),
+            pltpu.VMEM((256, HALF), BF16),
+            pltpu.VMEM((256, HALF), BF16),
+            pltpu.VMEM((RHS, 256), F32),
             pltpu.VMEM((len(CHAIN), 2, PART, 128), F32),
             pltpu.VMEM((2, PART, 128), F32),
             pltpu.VMEM((SLC, HALF), F32),

time: 73.1 us -> 71.3 us (0.975)
  the two profiles are of different devices: /device:TPU:35 before, /device:TPU:6 now
where the time goes in v5:
time: 71.3 us; the launch traced here: 70.6 us
  Pallas kernels  68.6 us (96%)
    pallas_call x1, Pallas kernels, body(): pl.pallas_call(kernel, out_shape=(pltpu.VMEM((STEPS, RHS, SLC), F32), plt...  68.6 us

profile of v5, /device:TPU:6, one launch (start us, length us, event | category | flops | bytes accessed | tf_op | source)
XLA Modules:
  0.0 70.6 jit_solution(15349219286281725495)
XLA Ops:
  0.6 68.6 %solve.1 = (f32[4,48,96]{2,1,0:T(8,128)S(1)}, f32[48,96]{1,0:T(8,128)S(1)}) custom-call(f32[4608,128]{1,0:T(8,128)} %bitcast.7, f32[4,96,1536]{2,1,0:T(8,128)} %inverse_ref.1, f32[576,128]{1,0:T(8,128)} %bitcast.8), custom_call_target="tpu_custom_call" | custom-call | tf_op jit(solution)/shard_map/solve/pallas_call | solution.py:644
  69.3 0.7 copy.5
  70.0 0.6 neg.6

commit v6 on v5

--- a/solution.py
+++ b/solution.py
@@ -141,28 +141,10 @@
         part = pl.ds(k * SLC * TILES, SLC * TILES)
         return pltpu.make_async_copy(panel_ref.at[part], flat.at[part], panel_sem.at[k])
 
-    load_right = pltpu.make_async_copy(right_ref, right_flat, right_sem)
-    load_right.start()
-
-    @pl.when(q == 0)
-    def _():
-        load_inverse(0).start()
-
-    for k in range(STEPS):
-        load_panel(k).start()
-
     barrier = pltpu.get_barrier_semaphore()
 
     def hello(row, col):
         pl.semaphore_signal(barrier, inc=1, device_id=(row, col), device_id_type=MESH)
-
-    @pl.when(q == 1)
-    def _():
-        hello(p, 0)
-
-    @pl.when(is_chain | (q == 3))
-    def _():
-        hello(p, 1)
 
     @pl.when(is_chain)
     def _():
@@ -172,6 +154,30 @@
 
         lax.fori_loop(0, ROWS - 1, ring, 0)
         hello(pair, q + 1)
+
+    load_right = pltpu.make_async_copy(right_ref, right_flat, right_sem)
+    load_right.start()
+
+    @pl.when(q == 0)
+    def _():
+        load_inverse(0).start()
+
+    @pl.when(q == 1)
+    def _():
+        load_panel(0).start()
+
+    @pl.when(q > 1)
+    def _():
+        for k in range(STEPS):
+            load_panel(k).start()
+
+    @pl.when(q == 1)
+    def _():
+        hello(p, 0)
+
+    @pl.when(is_chain | (q == 3))
+    def _():
+        hello(p, 1)
 
     @pl.when((q > 2) & jnp.logical_not(is_chain))
     def _():
@@ -236,6 +242,7 @@
         pieces[0, :, 0:SLC] = dot3(right[...], split(inv[0]), 1)
         pl.semaphore_wait(barrier, 1)
         push(pieces.at[0], pieces.at[0], first_send, piece_recv.at[0], (p, 1))
+        load_panel(0).start()
 
     @pl.when(q == 1)
     def _():
@@ -246,6 +253,11 @@
         base[...] = own * right[...] - dot3(pieces[0, :, 0:SLC], block(0), 0)
         send_base(1)
         push(pieces.at[0], pieces.at[0], first_send, piece_recv.at[0], (p, 3))
+
+    @pl.when(q < 2)
+    def _():
+        for k in range(1, STEPS):
+            load_panel(k).start()
 
     def send_block(k):
         for n in range(3):

time: 71.3 us -> 71.3 us (level)
  no operation moved by 1% of the time
where the time goes in v6:
time: 71.3 us; the launch traced here: 70.6 us
  Pallas kernels  68.7 us (96%)
    pallas_call x1, Pallas kernels, body(): pl.pallas_call(kernel, out_shape=(pltpu.VMEM((STEPS, RHS, SLC), F32), plt...  68.7 us

profile of v6, /device:TPU:6, one launch (start us, length us, event | category | flops | bytes accessed | tf_op | source)
XLA Modules:
  0.0 70.6 jit_solution(3466182500921724980)
XLA Ops:
  0.6 68.7 %solve.1 = (f32[4,48,96]{2,1,0:T(8,128)S(1)}, f32[48,96]{1,0:T(8,128)S(1)}) custom-call(f32[4608,128]{1,0:T(8,128)} %bitcast.7, f32[4,96,1536]{2,1,0:T(8,128)} %inverse_ref.1, f32[576,128]{1,0:T(8,128)} %bitcast.8), custom_call_target="tpu_custom_call" | custom-call | tf_op jit(solution)/shard_map/solve/pallas_call | solution.py:656
  69.3 0.7 copy.5
  70.0 0.6 neg.6
